TPU v7x, 32 devices: a whole 2x2x4 slice. The times are simulated.
32 devices in a mesh: dp: 8 (over y, x, core), tensor: 4 (over z).
Axes of the slice: x: 2, y: 2, z: 4, core: 2. Of those that a mesh axis runs over, the one named last changes fastest.
Arguments:
- tokens: bfloat16 [16, 1024, 1024], P('dp', 'tensor'), may hold values from -6 to 6
- segments: int32 [16, 1024], P('dp'), may hold values from 0 to 3, as said below
- qkv_weight: bfloat16 [3, 1024, 1024], P(None, None, 'tensor'), may hold values from -0.1875 to 0.1875
- qkv_bias: float32 [3, 1024], P(None, 'tensor'), may hold values from -1.5 to 1.5
- out_weight: bfloat16 [1024, 1024], P('tensor'), may hold values from -0.75 to 0.75
- out_bias: float32 [1024], replicated, may hold values from -1.5 to 1.5
- gain_one: float32 [1024], replicated, may hold values from 0.5 to 1.5
- shift_one: float32 [1024], replicated, may hold values from -1.5 to 1.5
- up_weight: bfloat16 [1024, 4096], P(None, 'tensor'), may hold values from -0.1875 to 0.1875
- up_bias: float32 [4096], P('tensor'), may hold values from -1.5 to 1.5
- down_weight: bfloat16 [4096, 1024], P('tensor'), may hold values from -0.1875 to 0.1875
- down_bias: float32 [1024], replicated, may hold values from -1.5 to 1.5
- gain_two: float32 [1024], replicated, may hold values from 0.5 to 1.5
- shift_two: float32 [1024], replicated, may hold values from -1.5 to 1.5
- proj_weight: bfloat16 [1024, 288], replicated, may hold values from -0.1875 to 0.1875
- out_grad: bfloat16 [16, 1024, 1024], P('dp', 'tensor'), may hold values from -6 to 6
- embed_grad: bfloat16 [16, 1024, 288], P('dp', 'tensor'), may hold values from -6 to 6
Outputs:
- layer_out: bfloat16 [16, 1024, 1024], P('dp', 'tensor')
- embeddings: bfloat16 [16, 1024, 288], P('dp', 'tensor')
- tokens_grad: float32 [16, 1024, 1024], P('dp', 'tensor')
- qkv_weight_grad: float32 [3, 1024, 1024], P(None, None, 'tensor')
- qkv_bias_grad: float32 [3, 1024], P(None, 'tensor')
- out_weight_grad: float32 [1024, 1024], P('tensor')
- out_bias_grad: float32 [1024], replicated
- gain_one_grad: float32 [1024], replicated
- shift_one_grad: float32 [1024], replicated
- up_weight_grad: float32 [1024, 4096], P(None, 'tensor')
- up_bias_grad: float32 [4096], P('tensor')
- down_weight_grad: float32 [4096, 1024], P('tensor')
- down_bias_grad: float32 [1024], replicated
- gain_two_grad: float32 [1024], replicated
- shift_two_grad: float32 [1024], replicated
- proj_weight_grad: float32 [1024, 288], replicated
Inputs may be any that keep to these rules, and one draw needn't show every extreme that they name: `segments`: segment numbers never fall along a sequence; every sequence holds 4 documents, each of at least 200 tokens, and in every sequence some document has exactly 200.
All inputs are finite; a program needn't handle non-finite values.
Results may differ from a plain program's by a relative error of at most 0.018.
Values may be sent and summed in bfloat16 or wider, within the bound.
A program may use at most 192 MiB of HBM per device.

v0:
```python
import math
import jax
import jax.numpy as jnp
from jax import lax
from jax.sharding import PartitionSpec as P

HEAD_DIM = 64
eps = 1e-05


def as_sent(array):

    def short(part):
        return part.astype(jnp.bfloat16) if part.dtype == jnp.float32 else part

    return jax.tree.map(short, array)


def doc_positions(segment_rows):
    length = segment_rows.shape[-1]
    row_index = jnp.broadcast_to(jnp.arange(length, dtype=jnp.int32), segment_rows.shape)
    change = jnp.concatenate(
        [
            jnp.ones(segment_rows.shape[:-1] + (1,), jnp.bool_),
            segment_rows[..., 1:] != segment_rows[..., :-1],
        ],
        axis=-1,
    )
    doc_start = lax.cummax(
        jnp.where(change, row_index, jnp.zeros_like(row_index)), axis=segment_rows.ndim - 1
    )
    return row_index - doc_start


def rotary_tables(positions, head_dim):
    half_dim = head_dim // 2
    exponent = jnp.arange(half_dim, dtype=jnp.float32) * (2.0 / head_dim)
    frequency = jnp.exp(-exponent * math.log(10000.0))
    angles = positions.astype(jnp.float32)[..., None] * frequency
    angles = jnp.concatenate([angles, angles], axis=-1)
    return (jnp.cos(angles), jnp.sin(angles))


def rotate(field, cosine, sine):
    half_dim = field.shape[-1] // 2
    rotated = jnp.concatenate([-field[..., half_dim:], field[..., :half_dim]], axis=-1)
    return field * cosine + rotated * sine


def rotate_back(field, cosine, sine):
    half_dim = field.shape[-1] // 2
    rotated = jnp.concatenate([-field[..., half_dim:], field[..., :half_dim]], axis=-1)
    return field * cosine - rotated * sine


def norm_forward(field, gain, shift):
    row_mean = jnp.mean(field, axis=-1, keepdims=True)
    centred = field - row_mean
    variance = jnp.mean(centred * centred, axis=-1, keepdims=True)
    inv_std = lax.rsqrt(variance + eps)
    scaled = centred * inv_std
    return (scaled * gain + shift, scaled, inv_std)


def norm_backward(upstream, scaled, inv_std, gain):
    grad_scaled = upstream * gain
    grad_input = inv_std * (
        grad_scaled
        - jnp.mean(grad_scaled, axis=-1, keepdims=True)
        - scaled * jnp.mean(grad_scaled * scaled, axis=-1, keepdims=True)
    )
    return (grad_input, jnp.sum(upstream * scaled, axis=(0, 1)), jnp.sum(upstream, axis=(0, 1)))


def device_rows(full_rows, row_count):
    groups, length, model_width = full_rows.shape
    local_rows = length // lax.axis_size("tensor")
    blocks = row_count // (groups * local_rows)
    picked = full_rows
    picked = picked.reshape(groups, blocks, local_rows, model_width).transpose(1, 0, 2, 3)
    return picked.reshape(row_count, model_width)


def masked_scores(queries, keys, seg_row):
    scores = jnp.einsum("hqd,hkd->hqk", queries, keys, preferred_element_type=jnp.float32)
    same_doc = seg_row[:, None] == seg_row[None, :]
    return jnp.where(same_doc[None], scores, -1000000000.0)


def attend(inputs):
    queries, keys, values_low, seg_row = inputs
    scores = masked_scores(queries, keys, seg_row)
    row_peak = jnp.max(scores, axis=-1, keepdims=True)
    shifted = jnp.exp(scores - row_peak)
    row_total = jnp.sum(shifted, axis=-1, keepdims=True)
    probs = (shifted / row_total).astype(jnp.bfloat16)
    mixed_heads = jnp.einsum("hqk,hkd->hqd", probs, values_low, preferred_element_type=jnp.float32)
    return (mixed_heads, row_peak + jnp.log(row_total))


def attend_back(inputs):
    queries, keys, values_low, seg_row, log_total, grad_mixed = inputs
    scores = masked_scores(queries, keys, seg_row)
    probs = jnp.exp(scores - log_total)
    grad_values = jnp.einsum(
        "hqk,hqd->hkd", probs.astype(jnp.bfloat16), grad_mixed, preferred_element_type=jnp.float32
    )
    grad_probs = jnp.einsum(
        "hqd,hkd->hqk", grad_mixed, values_low, preferred_element_type=jnp.float32
    )
    row_inner = jnp.sum(probs * grad_probs, axis=-1, keepdims=True)
    grad_scores = (probs * (grad_probs - row_inner)).astype(jnp.bfloat16)
    grad_queries = jnp.einsum("hqk,hkd->hqd", grad_scores, keys, preferred_element_type=jnp.float32)
    grad_keys = jnp.einsum("hqk,hqd->hkd", grad_scores, queries, preferred_element_type=jnp.float32)
    return (grad_queries, grad_keys, grad_values)


def process(tokens, segments, out_grad, embed_grad, weights):
    (
        qkv_weight,
        qkv_bias,
        out_weight,
        out_bias,
        gain_one,
        shift_one,
        up_weight,
        up_bias,
        down_weight,
        down_bias,
        gain_two,
        shift_two,
        proj_weight,
    ) = weights
    groups, local_rows, model_width = tokens.shape
    length = segments.shape[1]
    heads_here = qkv_weight.shape[2] // HEAD_DIM
    q_scale = HEAD_DIM ** (-0.5)
    cosine, sine = rotary_tables(doc_positions(segments), HEAD_DIM)
    cosine = cosine[:, None]
    sine = sine[:, None]

    def split_heads(field):
        return field.reshape(groups, length, heads_here, HEAD_DIM).transpose(0, 2, 1, 3)

    def join_heads(field):
        return field.transpose(0, 2, 1, 3).reshape(groups, length, heads_here * HEAD_DIM)

    whole_tokens = lax.all_gather(tokens, "tensor", axis=1, tiled=True)
    projected = jnp.einsum(
        "gld,cde->cgle", whole_tokens, qkv_weight, preferred_element_type=jnp.float32
    )
    projected = projected + qkv_bias[:, None, None, :]
    queries = (rotate(split_heads(projected[0]), cosine, sine) * q_scale).astype(jnp.bfloat16)
    keys = rotate(split_heads(projected[1]), cosine, sine).astype(jnp.bfloat16)
    values_low = split_heads(projected[2]).astype(jnp.bfloat16)
    mixed_heads, log_total = lax.map(attend, (queries, keys, values_low, segments))
    mixed = join_heads(mixed_heads).astype(jnp.bfloat16)
    attn_part = lax.psum_scatter(
        jnp.dot(
            device_rows(mixed, lax.axis_size("tensor") * (groups * local_rows)),
            out_weight,
            preferred_element_type=jnp.float32,
        ),
        "tensor",
        scatter_dimension=0,
        tiled=True,
    )
    attn_part = attn_part.reshape(groups, local_rows, model_width)
    first_sum = tokens.astype(jnp.float32) + (attn_part + out_bias)
    normed, scaled_one, inv_one = norm_forward(first_sum, gain_one, shift_one)
    whole_normed = lax.all_gather(normed.astype(jnp.bfloat16), "tensor", axis=1, tiled=True)
    hidden = (
        jnp.einsum("gld,df->glf", whole_normed, up_weight, preferred_element_type=jnp.float32)
        + up_bias
    )
    active = jax.nn.gelu(hidden, approximate=False).astype(jnp.bfloat16)
    ffn_part = lax.psum_scatter(
        jnp.dot(
            device_rows(active, lax.axis_size("tensor") * (groups * local_rows)),
            down_weight,
            preferred_element_type=jnp.float32,
        ),
        "tensor",
        scatter_dimension=0,
        tiled=True,
    )
    second_sum = normed + (ffn_part.reshape(groups, local_rows, model_width) + down_bias)
    result, scaled_two, inv_two = norm_forward(second_sum, gain_two, shift_two)
    result_low = result.astype(jnp.bfloat16)
    embedded = jnp.einsum(
        "gld,dp->glp", result_low, proj_weight, preferred_element_type=jnp.float32
    )
    grad_result = out_grad.astype(jnp.float32) + jnp.einsum(
        "glp,dp->gld", embed_grad, proj_weight, preferred_element_type=jnp.float32
    )
    proj_grad = jnp.einsum(
        "gld,glp->dp", result_low, embed_grad, preferred_element_type=jnp.float32
    )
    grad_second, gain_two_grad, shift_two_grad = norm_backward(
        grad_result, scaled_two, inv_two, gain_two
    )
    second_low = grad_second.astype(jnp.bfloat16)
    down_bias_grad = jnp.sum(second_low.astype(jnp.float32), axis=(0, 1))
    whole_second = lax.all_gather(second_low, "tensor", axis=1, tiled=True)
    down_weight_grad = jnp.einsum(
        "glf,gld->fd", active, whole_second, preferred_element_type=jnp.float32
    )
    grad_active = jnp.einsum(
        "gld,fd->glf", whole_second, down_weight, preferred_element_type=jnp.float32
    )
    gelu_pull = jax.vjp(lambda field: jax.nn.gelu(field, approximate=False), hidden)[1]
    grad_hidden = gelu_pull(grad_active)[0].astype(jnp.bfloat16)
    up_bias_grad = jnp.sum(grad_hidden.astype(jnp.float32), axis=(0, 1))
    up_weight_grad = jnp.einsum(
        "gld,glf->df", whole_normed, grad_hidden, preferred_element_type=jnp.float32
    )
    ffn_back = lax.psum_scatter(
        jnp.einsum(
            "nf,df->nd",
            device_rows(grad_hidden, lax.axis_size("tensor") * (groups * local_rows)),
            up_weight,
            preferred_element_type=jnp.float32,
        ),
        "tensor",
        scatter_dimension=0,
        tiled=True,
    )
    grad_normed = grad_second + ffn_back.reshape(groups, local_rows, model_width)
    grad_first, gain_one_grad, shift_one_grad = norm_backward(
        grad_normed, scaled_one, inv_one, gain_one
    )
    first_low = grad_first.astype(jnp.bfloat16)
    out_bias_grad = jnp.sum(first_low.astype(jnp.float32), axis=(0, 1))
    whole_first = lax.all_gather(first_low, "tensor", axis=1, tiled=True)
    out_weight_grad = jnp.einsum(
        "glh,gld->hd", mixed, whole_first, preferred_element_type=jnp.float32
    )
    grad_mixed = jnp.einsum(
        "gld,hd->glh", whole_first, out_weight, preferred_element_type=jnp.float32
    )
    grad_mixed = split_heads(grad_mixed.astype(jnp.bfloat16))
    grad_queries, grad_keys, grad_values = lax.map(
        attend_back, (queries, keys, values_low, segments, log_total, grad_mixed)
    )
    grad_queries = rotate_back(grad_queries * q_scale, cosine, sine)
    grad_keys = rotate_back(grad_keys, cosine, sine)
    grad_qkv = jnp.stack(
        [join_heads(grad_queries), join_heads(grad_keys), join_heads(grad_values)]
    ).astype(jnp.bfloat16)
    qkv_bias_grad = jnp.sum(grad_qkv.astype(jnp.float32), axis=(1, 2))
    qkv_weight_grad = jnp.einsum(
        "gld,cgle->cde", whole_tokens, grad_qkv, preferred_element_type=jnp.float32
    )
    joined_grad = grad_qkv.transpose(1, 2, 0, 3).reshape(groups, length, 3 * heads_here * HEAD_DIM)
    joined_weight = qkv_weight.transpose(1, 0, 2).reshape(model_width, 3 * heads_here * HEAD_DIM)
    input_back = lax.psum_scatter(
        jnp.einsum(
            "ne,de->nd",
            device_rows(joined_grad, groups * local_rows * lax.axis_size("tensor")),
            joined_weight,
            preferred_element_type=jnp.float32,
        ).astype(jnp.bfloat16),
        "tensor",
        scatter_dimension=0,
        tiled=True,
    ).astype(jnp.float32)
    tokens_grad = grad_first + input_back.reshape(groups, local_rows, model_width)
    sharded_grads = (
        qkv_weight_grad,
        qkv_bias_grad,
        out_weight_grad,
        up_weight_grad,
        up_bias_grad,
        down_weight_grad,
    )
    shared_grads = (
        out_bias_grad,
        gain_one_grad,
        shift_one_grad,
        down_bias_grad,
        gain_two_grad,
        shift_two_grad,
        proj_grad,
    )
    return (result_low, embedded.astype(jnp.bfloat16), tokens_grad, sharded_grads, shared_grads)


def per_device(
    tokens,
    segments,
    qkv_weight,
    qkv_bias,
    out_weight,
    out_bias,
    gain_one,
    shift_one,
    up_weight,
    up_bias,
    down_weight,
    down_bias,
    gain_two,
    shift_two,
    proj_weight,
    out_grad,
    embed_grad,
):
    weights = (
        qkv_weight,
        qkv_bias,
        out_weight,
        out_bias,
        gain_one,
        shift_one,
        up_weight,
        up_bias,
        down_weight,
        down_bias,
        gain_two,
        shift_two,
        proj_weight,
    )

    def one_seq(running, per_seq):
        tok_row, seg_row, dy_row, de_row = per_seq
        results = process(tok_row[None], seg_row[None], dy_row[None], de_row[None], weights)
        running = jax.tree.map(jnp.add, running, (results[3], results[4]))
        return (running, (results[0][0], results[1][0], results[2][0]))

    empty_grads = (
        tuple(
            (
                jnp.zeros(w.shape, jnp.float32)
                for w in (qkv_weight, qkv_bias, out_weight, up_weight, up_bias, down_weight)
            )
        ),
        tuple(
            (
                jnp.zeros(w.shape, jnp.float32)
                for w in (
                    out_bias,
                    gain_one,
                    shift_one,
                    down_bias,
                    gain_two,
                    shift_two,
                    proj_weight,
                )
            )
        ),
    )
    (sharded_grads, shared_grads), (layer_out, embeddings, tokens_grad) = lax.scan(
        one_seq, empty_grads, (tokens, segments, out_grad, embed_grad)
    )
    sharded_grads = jax.tree.map(
        lambda part: part.astype(jnp.float32), lax.psum(as_sent(sharded_grads), "dp")
    )
    shared_grads = lax.psum(shared_grads, ("dp", "tensor"))
    return (
        layer_out,
        embeddings,
        tokens_grad,
        sharded_grads[0],
        sharded_grads[1],
        sharded_grads[2],
        shared_grads[0],
        shared_grads[1],
        shared_grads[2],
        sharded_grads[3],
        sharded_grads[4],
        sharded_grads[5],
        shared_grads[3],
        shared_grads[4],
        shared_grads[5],
        shared_grads[6],
    )


def solution(mesh):
    in_specs = (
        P("dp", "tensor", None),
        P("dp", None),
        P(None, None, "tensor"),
        P(None, "tensor"),
        P("tensor", None),
        P(),
        P(),
        P(),
        P(None, "tensor"),
        P("tensor"),
        P("tensor", None),
        P(),
        P(),
        P(),
        P(),
        P("dp", "tensor", None),
        P("dp", "tensor", None),
    )
    out_specs = (
        P("dp", "tensor", None),
        P("dp", "tensor", None),
        P("dp", "tensor", None),
        P(None, None, "tensor"),
        P(None, "tensor"),
        P("tensor", None),
        P(),
        P(),
        P(),
        P(None, "tensor"),
        P("tensor"),
        P("tensor", None),
        P(),
        P(),
        P(),
        P(),
    )
    return jax.shard_map(
        per_device, mesh=mesh, in_specs=in_specs, out_specs=out_specs, check_vma=False
    )
```

profile of v0, /device:TPU:0, one launch (start us, length us, event | category | flops | bytes accessed | tf_op | source)
XLA Modules:
  0.0 1448.8 jit_solution(7580111649799563815)
XLA Ops:
  10.8 1174.9 %while.6 = (s32[]{:T(128)}, f32[3,1024,256]{1,2,0:T(8,128)}, f32[3,256]{1,0:T(4,128)}, f32[256,1024]{1,0:T(8,128)}, f32[1024,1024]{1,0:T(8,128)}, /*index=5*/f32...) while((s32[]{:T(128)}, f32[3,1024,256]{1,2,0:T(8,128)}, ...), condition=%wide.region_26.27_spmd.clone, body=%wide.region_0.26_spmd.clone.sunk | while | flops 23216961536 | bytes 635246848 | solution.py:351
  17.6 44.3 %all-gather.5.cloned.1.call-done = bf16[1,1024,1024]{2,1,0:T(8,128)(2,1)} async-done(((bf16[1,256,1024]{2,1,0:T(8,128)(2,1)}), bf16[1,1024,1024]{2,1,0:T(8,128)(2,1)}) %all-gather.5.cloned.1.call-update) | async-done | bytes 2097168 | tf_op jit(solution)/shard_map/while/body/eval_jaxpr/all_gather | solution.py:148
  74.1 8.8 fusion.227
  95.1 75.3 %reduce-scatter.5.cloned.1.call-done = f32[256,1024]{1,0:T(8,128)} async-done(((f32[1024,1024]{1,0:T(8,128)}), f32[256,1024]{1,0:T(8,128)}) %reduce-scatter.5.cloned.1.call-update) | async-done | bytes 1048592 | tf_op jit(solution)/shard_map/while/body/eval_jaxpr/reduce_scatter | solution.py:158
  173.2 46.6 %all-gather.7.cloned.1.call-done = bf16[1,1024,1024]{2,1,0:T(8,128)(2,1)} async-done(((bf16[1,256,1024]{2,1,0:T(8,128)(2,1)}), bf16[1,1024,1024]{2,1,0:T(8,128)(2,1)}) %all-gather.7.cloned.1.call-update) | async-done | bytes 2097168 | tf_op jit(solution)/shard_map/while/body/eval_jaxpr/all_gather | solution.py:171
  219.8 14.8 %multiply_convert_fusion.4 = (bf16[1024,1024]{1,0:T(8,128)(2,1)S(1)}, f32[1024,1024]{1,0:T(8,128)}, f32[1024,1024]{1,0:T(8,128)}) fusion(f32[1024]{0:T(1024)S(1)} %copy-done.58, bf16[1024,1024]{1,0:T(8,128)(2,1)} %get-tuple-element.999, bf16[1,1024,1024]{2,1,0:T(8,128)(2,1)} %all-gather.7.cloned.1.call-done), kind=kOutput, calls=%fused_computation.17.clone.1 | convolution fusion | flops 2216689664 | bytes 14684160 | tf_op jit(solution)/shard_map/while/body/eval_jaxpr/gld,df->glf/dot_general | solution.py:173
  240.3 75.6 %reduce-scatter.7.cloned.1.call-done = f32[256,1024]{1,0:T(8,128)} async-done(((f32[1024,1024]{1,0:T(8,128)}), f32[256,1024]{1,0:T(8,128)}) %reduce-scatter.7.cloned.1.call-update) | async-done | bytes 1048592 | tf_op jit(solution)/shard_map/while/body/eval_jaxpr/reduce_scatter | solution.py:177
  322.1 46.0 %all-gather.9.cloned.1.call-done = bf16[1,1024,1024]{2,1,0:T(8,128)(2,1)} async-done(((bf16[1,256,1024]{2,1,0:T(8,128)(2,1)}), bf16[1,1024,1024]{2,1,0:T(8,128)(2,1)}) %all-gather.9.cloned.1.call-update) | async-done | bytes 2097168 | tf_op jit(solution)/shard_map/while/body/eval_jaxpr/all_gather | solution.py:204
  368.0 8.5 convert_reduce_fusion.9
  382.3 75.6 %reduce-scatter.9.cloned.1.call-done = f32[256,1024]{1,0:T(8,128)} async-done(((f32[1024,1024]{1,0:T(8,128)}), f32[256,1024]{1,0:T(8,128)}) %reduce-scatter.9.cloned.1.call-update) | async-done | bytes 1048592 | tf_op jit(solution)/shard_map/while/body/eval_jaxpr/reduce_scatter | solution.py:217
  461.7 46.5 %all-gather.11.cloned.1.call-done = bf16[1,1024,1024]{2,1,0:T(8,128)(2,1)} async-done(((bf16[1,256,1024]{2,1,0:T(8,128)(2,1)}), bf16[1,1024,1024]{2,1,0:T(8,128)(2,1)}) %all-gather.11.cloned.1.call-update) | async-done | bytes 2097168 | tf_op jit(solution)/shard_map/while/body/eval_jaxpr/all_gather | solution.py:234
  510.6 8.7 fusion.236
  519.4 11.8 multiply_reduce_fusion.18
  531.2 12.2 multiply_convert_fusion.5
  576.4 19.7 %reduce-scatter.11.cloned.1.call-done = bf16[256,1024]{1,0:T(8,128)(2,1)} async-done(((bf16[1024,1024]{1,0:T(8,128)(2,1)}), bf16[256,1024]{1,0:T(8,128)(2,1)}) %reduce-scatter.11.cloned.1.call-update) | async-done | bytes 524304 | tf_op jit(solution)/shard_map/while/body/eval_jaxpr/reduce_scatter | solution.py:256
  605.3 40.9 %all-gather.5.cloned.1.call-done = bf16[1,1024,1024]{2,1,0:T(8,128)(2,1)} async-done(((bf16[1,256,1024]{2,1,0:T(8,128)(2,1)}), bf16[1,1024,1024]{2,1,0:T(8,128)(2,1)}) %all-gather.5.cloned.1.call-update) | async-done | bytes 2097168 | tf_op jit(solution)/shard_map/while/body/eval_jaxpr/all_gather | solution.py:148
  658.5 8.8 fusion.227
  679.5 75.1 %reduce-scatter.5.cloned.1.call-done = f32[256,1024]{1,0:T(8,128)} async-done(((f32[1024,1024]{1,0:T(8,128)}), f32[256,1024]{1,0:T(8,128)}) %reduce-scatter.5.cloned.1.call-update) | async-done | bytes 1048592 | tf_op jit(solution)/shard_map/while/body/eval_jaxpr/reduce_scatter | solution.py:158
  757.5 46.6 %all-gather.7.cloned.1.call-done = bf16[1,1024,1024]{2,1,0:T(8,128)(2,1)} async-done(((bf16[1,256,1024]{2,1,0:T(8,128)(2,1)}), bf16[1,1024,1024]{2,1,0:T(8,128)(2,1)}) %all-gather.7.cloned.1.call-update) | async-done | bytes 2097168 | tf_op jit(solution)/shard_map/while/body/eval_jaxpr/all_gather | solution.py:171
  804.1 14.8 %multiply_convert_fusion.4 = (bf16[1024,1024]{1,0:T(8,128)(2,1)S(1)}, f32[1024,1024]{1,0:T(8,128)}, f32[1024,1024]{1,0:T(8,128)}) fusion(f32[1024]{0:T(1024)S(1)} %copy-done.58, bf16[1024,1024]{1,0:T(8,128)(2,1)} %get-tuple-element.999, bf16[1,1024,1024]{2,1,0:T(8,128)(2,1)} %all-gather.7.cloned.1.call-done), kind=kOutput, calls=%fused_computation.17.clone.1 | convolution fusion | flops 2216689664 | bytes 14684160 | tf_op jit(solution)/shard_map/while/body/eval_jaxpr/gld,df->glf/dot_general | solution.py:173
  824.6 75.6 %reduce-scatter.7.cloned.1.call-done = f32[256,1024]{1,0:T(8,128)} async-done(((f32[1024,1024]{1,0:T(8,128)}), f32[256,1024]{1,0:T(8,128)}) %reduce-scatter.7.cloned.1.call-update) | async-done | bytes 1048592 | tf_op jit(solution)/shard_map/while/body/eval_jaxpr/reduce_scatter | solution.py:177
  906.0 46.4 %all-gather.9.cloned.1.call-done = bf16[1,1024,1024]{2,1,0:T(8,128)(2,1)} async-done(((bf16[1,256,1024]{2,1,0:T(8,128)(2,1)}), bf16[1,1024,1024]{2,1,0:T(8,128)(2,1)}) %all-gather.9.cloned.1.call-update) | async-done | bytes 2097168 | tf_op jit(solution)/shard_map/while/body/eval_jaxpr/all_gather | solution.py:204
  966.6 75.6 %reduce-scatter.9.cloned.1.call-done = f32[256,1024]{1,0:T(8,128)} async-done(((f32[1024,1024]{1,0:T(8,128)}), f32[256,1024]{1,0:T(8,128)}) %reduce-scatter.9.cloned.1.call-update) | async-done | bytes 1048592 | tf_op jit(solution)/shard_map/while/body/eval_jaxpr/reduce_scatter | solution.py:217
  1046.0 46.5 %all-gather.11.cloned.1.call-done = bf16[1,1024,1024]{2,1,0:T(8,128)(2,1)} async-done(((bf16[1,256,1024]{2,1,0:T(8,128)(2,1)}), bf16[1,1024,1024]{2,1,0:T(8,128)(2,1)}) %all-gather.11.cloned.1.call-update) | async-done | bytes 2097168 | tf_op jit(solution)/shard_map/while/body/eval_jaxpr/all_gather | solution.py:234
  1095.0 8.7 fusion.236
  1103.7 11.8 multiply_reduce_fusion.18
  1115.5 12.3 multiply_convert_fusion.5
  1163.0 17.5 %reduce-scatter.11.cloned.1.call-done = bf16[256,1024]{1,0:T(8,128)(2,1)} async-done(((bf16[1024,1024]{1,0:T(8,128)(2,1)}), bf16[256,1024]{1,0:T(8,128)(2,1)}) %reduce-scatter.11.cloned.1.call-update) | async-done | bytes 524304 | tf_op jit(solution)/shard_map/while/body/eval_jaxpr/reduce_scatter | solution.py:256
  1197.3 13.8 all-reduce.1
  1212.2 40.5 %all-reduce = (f32[1024]{0:T(1024)}, f32[1024]{0:T(1024)}, f32[1024]{0:T(1024)}, f32[1024]{0:T(1024)}, f32[1024]{0:T(1024)}, /*index=5*/f32[1024]{0:T(1024)}) all-reduce(f32[1024]{0:T(1024)S(1)} %copy-done.49, f32[1024]{0:T(1024)S(1)} %copy-done.46, f32[1024]{0:T(1024)S(1)} %copy-done.43, ...), channel_id=1, replica_groups=mesh['dp'=8,'tensor'=4] {'dp','tensor'}, use_global_device_ids=true, to_apply=%region_30.31 | all-reduce | flops 6144 | bytes 49152 | tf_op jit(solution)/shard_map/psum | solution.py:357
  1252.7 48.6 %all-reduce.8.cloned.1.call-done = (bf16[3,1024,256]{2,1,0:T(8,128)(2,1)}, bf16[256,1024]{1,0:T(8,128)(2,1)}, bf16[1024,1024]{1,0:T(8,128)(2,1)}, bf16[1024,1024]{1,0:T(8,128)(2,1)}) async-done(((bf16[3,1024,256]{2,1,0:T(8,128)(2,1)}, bf16[256,1024]{1,0:T(8,128)(2,1)}, bf16[1024,1024]{1,0:T(8,128)(2,1)}, bf16[1024,1024]{1,0:T(8,128)(2,1)}), (bf16[3,1024,256]{2,1,0:T(8,128)(2,1)}, ...) | async-done | bytes 6291472 | tf_op jit(solution)/shard_map/psum | solution.py:355
  1311.9 127.1 %all-reduce.6.cloned.1.call-done = f32[1024,288]{0,1:T(8,128)} async-done(((f32[1024,288]{0,1:T(8,128)}), f32[1024,288]{0,1:T(8,128)}) %all-reduce.6.cloned.1.call-update) | async-done | bytes 1179664 | tf_op jit(solution)/shard_map/psum | solution.py:357
  (429 shorter events, 223.2 us)
Async XLA Ops:
  10.8 51.1 %all-gather.5.cloned.1.call-start = ((), (), s32[]{:S(2)}) async-start(), calls=%async_computation.6 | async-start | bytes 2621440 | tf_op jit(solution)/shard_map/while/body/eval_jaxpr/all_gather | solution.py:148
  12.7 157.6 %reduce-scatter.5.cloned.1.call-start = ((), (), s32[]{:S(2)}) async-start(), calls=%async_computation.7 | async-start | bytes 5242880 | tf_op jit(solution)/shard_map/while/body/eval_jaxpr/reduce_scatter | solution.py:158
  94.6 75.7 %copy-start.17 = (bf16[2,256,1024]{2,1,0:T(8,128)(2,1)S(1)}, bf16[2,256,1024]{2,1,0:T(8,128)(2,1)}, u32[]{:S(2)}) copy-start(bf16[2,256,1024]{2,1,0:T(8,128)(2,1)} %get-tuple-element.992) | copy-start | bytes 3145732 | tf_op jit(solution)/shard_map/while
  94.6 75.7 %copy-start.50 = (f32[1024]{0:T(1024)S(1)}, f32[1024]{0:T(1024)}, u32[]{:S(2)}) copy-start(f32[1024]{0:T(1024)} %get-tuple-element.996) | copy-start | bytes 12292 | tf_op jit(solution)/shard_map/while
  94.6 77.4 %copy-start.28 = (f32[1024]{0:T(1024)S(1)}, f32[1024]{0:T(1024)}, u32[]{:S(2)}) copy-start(f32[1024]{0:T(1024)} %get-tuple-element.997) | copy-start | bytes 12292 | tf_op jit(solution)/shard_map/while
  94.6 77.4 %copy-start.30 = (f32[1024]{0:T(1024)S(1)}, f32[1024]{0:T(1024)}, u32[]{:S(2)}) copy-start(f32[1024]{0:T(1024)} %get-tuple-element.998) | copy-start | bytes 12292 | tf_op jit(solution)/shard_map/while
  94.6 125.1 %copy-start.58 = (f32[1024]{0:T(1024)S(1)}, f32[1024]{0:T(1024)}, u32[]{:S(2)}) copy-start(f32[1024]{0:T(1024)} %get-tuple-element.1000) | copy-start | bytes 12292 | tf_op jit(solution)/shard_map/while
  94.7 125.1 %all-gather.7.cloned.1.call-start = ((), (), s32[]{:S(2)}) async-start(), calls=%async_computation.8 | async-start | bytes 2621440 | tf_op jit(solution)/shard_map/while/body/eval_jaxpr/all_gather | solution.py:171
  173.1 142.7 %reduce-scatter.7.cloned.1.call-start = ((), (), s32[]{:S(2)}) async-start(), calls=%async_computation.9 | async-start | bytes 5242880 | tf_op jit(solution)/shard_map/while/body/eval_jaxpr/reduce_scatter | solution.py:177
  240.2 75.7 %copy-start.51 = (f32[1024]{0:T(1024)S(1)}, f32[1024]{0:T(1024)}, u32[]{:S(2)}) copy-start(f32[1024]{0:T(1024)} %get-tuple-element.1002) | copy-start | bytes 12292 | tf_op jit(solution)/shard_map/while
  240.2 77.6 %copy-start.31 = (f32[1024]{0:T(1024)S(1)}, f32[1024]{0:T(1024)}, u32[]{:S(2)}) copy-start(f32[1024]{0:T(1024)} %get-tuple-element.1006) | copy-start | bytes 12292 | tf_op jit(solution)/shard_map/while
  240.3 127.8 %all-gather.9.cloned.1.call-start = ((), (), s32[]{:S(2)}) async-start(), calls=%async_computation.10 | async-start | bytes 2621440 | tf_op jit(solution)/shard_map/while/body/eval_jaxpr/all_gather | solution.py:204
  321.4 136.4 %reduce-scatter.9.cloned.1.call-start = ((), (), s32[]{:S(2)}) async-start(), calls=%async_computation.11 | async-start | bytes 5242880 | tf_op jit(solution)/shard_map/while/body/eval_jaxpr/reduce_scatter | solution.py:217
  382.2 125.9 %all-gather.11.cloned.1.call-start = ((), (), s32[]{:S(2)}) async-start(), calls=%async_computation.12 | async-start | bytes 2621440 | tf_op jit(solution)/shard_map/while/body/eval_jaxpr/all_gather | solution.py:234
  461.6 134.5 %reduce-scatter.11.cloned.1.call-start = ((), (), s32[]{:S(2)}) async-start(), calls=%async_computation.13 | async-start | bytes 2621440 | tf_op jit(solution)/shard_map/while/body/eval_jaxpr/reduce_scatter | solution.py:256
  598.5 47.7 %all-gather.5.cloned.1.call-start = ((), (), s32[]{:S(2)}) async-start(), calls=%async_computation.6 | async-start | bytes 2621440 | tf_op jit(solution)/shard_map/while/body/eval_jaxpr/all_gather | solution.py:148
  600.5 154.2 %reduce-scatter.5.cloned.1.call-start = ((), (), s32[]{:S(2)}) async-start(), calls=%async_computation.7 | async-start | bytes 5242880 | tf_op jit(solution)/shard_map/while/body/eval_jaxpr/reduce_scatter | solution.py:158
  679.0 75.7 %copy-start.17 = (bf16[2,256,1024]{2,1,0:T(8,128)(2,1)S(1)}, bf16[2,256,1024]{2,1,0:T(8,128)(2,1)}, u32[]{:S(2)}) copy-start(bf16[2,256,1024]{2,1,0:T(8,128)(2,1)} %get-tuple-element.992) | copy-start | bytes 3145732 | tf_op jit(solution)/shard_map/while
  679.0 75.7 %copy-start.50 = (f32[1024]{0:T(1024)S(1)}, f32[1024]{0:T(1024)}, u32[]{:S(2)}) copy-start(f32[1024]{0:T(1024)} %get-tuple-element.996) | copy-start | bytes 12292 | tf_op jit(solution)/shard_map/while
  679.0 77.4 %copy-start.28 = (f32[1024]{0:T(1024)S(1)}, f32[1024]{0:T(1024)}, u32[]{:S(2)}) copy-start(f32[1024]{0:T(1024)} %get-tuple-element.997) | copy-start | bytes 12292 | tf_op jit(solution)/shard_map/while
  679.0 77.4 %copy-start.30 = (f32[1024]{0:T(1024)S(1)}, f32[1024]{0:T(1024)}, u32[]{:S(2)}) copy-start(f32[1024]{0:T(1024)} %get-tuple-element.998) | copy-start | bytes 12292 | tf_op jit(solution)/shard_map/while
  679.0 125.1 %copy-start.58 = (f32[1024]{0:T(1024)S(1)}, f32[1024]{0:T(1024)}, u32[]{:S(2)}) copy-start(f32[1024]{0:T(1024)} %get-tuple-element.1000) | copy-start | bytes 12292 | tf_op jit(solution)/shard_map/while
  679.0 125.1 %all-gather.7.cloned.1.call-start = ((), (), s32[]{:S(2)}) async-start(), calls=%async_computation.8 | async-start | bytes 2621440 | tf_op jit(solution)/shard_map/while/body/eval_jaxpr/all_gather | solution.py:171
  757.5 142.7 %reduce-scatter.7.cloned.1.call-start = ((), (), s32[]{:S(2)}) async-start(), calls=%async_computation.9 | async-start | bytes 5242880 | tf_op jit(solution)/shard_map/while/body/eval_jaxpr/reduce_scatter | solution.py:177
  824.6 75.7 %copy-start.51 = (f32[1024]{0:T(1024)S(1)}, f32[1024]{0:T(1024)}, u32[]{:S(2)}) copy-start(f32[1024]{0:T(1024)} %get-tuple-element.1002) | copy-start | bytes 12292 | tf_op jit(solution)/shard_map/while
  824.6 77.6 %copy-start.31 = (f32[1024]{0:T(1024)S(1)}, f32[1024]{0:T(1024)}, u32[]{:S(2)}) copy-start(f32[1024]{0:T(1024)} %get-tuple-element.1006) | copy-start | bytes 12292 | tf_op jit(solution)/shard_map/while
  824.6 127.8 %all-gather.9.cloned.1.call-start = ((), (), s32[]{:S(2)}) async-start(), calls=%async_computation.10 | async-start | bytes 2621440 | tf_op jit(solution)/shard_map/while/body/eval_jaxpr/all_gather | solution.py:204
  905.8 136.4 %reduce-scatter.9.cloned.1.call-start = ((), (), s32[]{:S(2)}) async-start(), calls=%async_computation.11 | async-start | bytes 5242880 | tf_op jit(solution)/shard_map/while/body/eval_jaxpr/reduce_scatter | solution.py:217
  966.6 125.9 %all-gather.11.cloned.1.call-start = ((), (), s32[]{:S(2)}) async-start(), calls=%async_computation.12 | async-start | bytes 2621440 | tf_op jit(solution)/shard_map/while/body/eval_jaxpr/all_gather | solution.py:234
  1045.9 134.6 %reduce-scatter.11.cloned.1.call-start = ((), (), s32[]{:S(2)}) async-start(), calls=%async_computation.13 | async-start | bytes 2621440 | tf_op jit(solution)/shard_map/while/body/eval_jaxpr/reduce_scatter | solution.py:256
  1185.7 115.6 %all-reduce.8.cloned.1.call-start = ((), (), s32[]{:S(2)}) async-start(), calls=%async_computation.5 | async-start | bytes 12582912 | tf_op jit(solution)/shard_map/psum | solution.py:355
  1196.6 242.5 %all-reduce.6.cloned.1.call-start = ((), (), s32[]{:S(2)}) async-start(), calls=%async_computation.4 | async-start | bytes 2359296 | tf_op jit(solution)/shard_map/psum | solution.py:357
  (101 other events, 699.8 us)
Sparse Core Ops, SparseCore 0:
  13.2 48.6 all-gather.4
  94.8 75.4 reduce-scatter.4
  173.3 46.4 all-gather.6
  240.4 75.4 reduce-scatter.6
  321.6 46.4 all-gather.8
  382.4 75.4 reduce-scatter.8
  461.7 46.4 all-gather.10
  553.5 42.5 reduce-scatter.10
  600.9 45.2 all-gather.4
  679.1 75.4 reduce-scatter.4
  757.6 46.4 all-gather.6
  824.7 75.4 reduce-scatter.6
  905.9 46.4 all-gather.8
  966.7 75.4 reduce-scatter.8
  1046.0 46.4 all-gather.10
  1137.9 42.5 reduce-scatter.10
Sparse Core Ops, SparseCore 1:
  1196.7 104.6 all-reduce.7
  1308.1 130.9 all-reduce.5
where the time goes:
time: 1450 us
  waiting for transfers between devices  1030 us (71%)
  matrix products  209 us (14%)
  other arithmetic  99.4 us (7%)
  blocking collectives  54.2 us (4%)
  local copies, waits for them, and re-layouts  33.1 us (2%)
  between operations  15.6 us (1%)
    reduce_scatter x2, waiting for transfers between devices, process(): lax.psum_scatter(jnp.einsum('nf,df->nd', device_rows(grad_hidden, lax.axi...  151 us
    reduce_scatter x2, waiting for transfers between devices, process(): lax.psum_scatter(jnp.dot(device_rows(active, lax.axis_size('tensor') * (g...  151 us
    reduce_scatter x2, waiting for transfers between devices, process(): lax.psum_scatter(jnp.dot(device_rows(mixed, lax.axis_size('tensor') * (gr...  150 us
    psum x1, waiting for transfers between devices, per_device(): shared_grads = lax.psum(shared_grads, ('dp', 'tensor'))  127 us
    all_gather x2, waiting for transfers between devices, process(): lax.all_gather(normed.astype(jnp.bfloat16), 'tensor', axis=1, tiled=True)  93.1 us
    all_gather x2, waiting for transfers between devices, process(): whole_first = lax.all_gather(first_low, 'tensor', axis=1, tiled=True)  93 us
    all_gather x2, waiting for transfers between devices, process(): whole_second = lax.all_gather(second_low, 'tensor', axis=1, tiled=True)  92.3 us
    all_gather x2, waiting for transfers between devices, process(): whole_tokens = lax.all_gather(tokens, 'tensor', axis=1, tiled=True)  85.2 us
  transfers between devices with their start and end apart: 18, of which 18 were waited for; matrix products, arithmetic and copies ran while one was open for 4% of the time, Pallas kernels for 0%

commit v1 on v0

--- a/solution.py
+++ b/solution.py
@@ -354,7 +354,7 @@
     sharded_grads = jax.tree.map(
         lambda part: part.astype(jnp.float32), lax.psum(as_sent(sharded_grads), "dp")
     )
-    shared_grads = lax.psum(shared_grads, ("dp", "tensor"))
+    shared_grads = lax.psum(lax.psum(shared_grads, "tensor"), "dp")
     return (
         layer_out,
         embeddings,

time: 1450 us -> 1430 us (0.986)
  waiting for transfers between devices: 1030 us -> 1000 us
    psum x1 -> x2, waiting for transfers between devices: 127 us -> 96.7 us  [per_device(): shared_grads = lax.psum(lax.psum(shared_grads, 'tensor'), 'dp')]
    psum x1 -> x2, blocking collectives: 40.5 us -> 41.2 us  [per_device(): shared_grads = lax.psum(lax.psum(shared_grads, 'tensor'), 'dp')]
  transfers between devices with their start and end apart: 18 -> 19, of which waited for: 18 -> 19; matrix products, arithmetic and copies ran while one was open for 4% -> 5% of each run, Pallas kernels for 0% -> 0%
where the time goes in v1:
time: 1430 us; the launch traced here: 1420 us
  waiting for transfers between devices  1000 us (70%)
  matrix products  209 us (15%)
  other arithmetic  99.4 us (7%)
  blocking collectives  54.5 us (4%)
  local copies, waits for them, and re-layouts  33.1 us (2%)
  between operations  15.8 us (1%)
    reduce_scatter x2, waiting for transfers between devices, process(): lax.psum_scatter(jnp.einsum('nf,df->nd', device_rows(grad_hidden, lax.axi...  151 us
    reduce_scatter x2, waiting for transfers between devices, process(): lax.psum_scatter(jnp.dot(device_rows(active, lax.axis_size('tensor') * (g...  151 us
    reduce_scatter x2, waiting for transfers between devices, process(): lax.psum_scatter(jnp.dot(device_rows(mixed, lax.axis_size('tensor') * (gr...  150 us
    psum x2, waiting for transfers between devices, per_device(): shared_grads = lax.psum(lax.psum(shared_grads, 'tensor'), 'dp')  96.7 us
    all_gather x2, waiting for transfers between devices, process(): lax.all_gather(normed.astype(jnp.bfloat16), 'tensor', axis=1, tiled=True)  93.1 us
    all_gather x2, waiting for transfers between devices, process(): whole_first = lax.all_gather(first_low, 'tensor', axis=1, tiled=True)  93 us
    all_gather x2, waiting for transfers between devices, process(): whole_second = lax.all_gather(second_low, 'tensor', axis=1, tiled=True)  92.3 us
    all_gather x2, waiting for transfers between devices, process(): whole_tokens = lax.all_gather(tokens, 'tensor', axis=1, tiled=True)  85.2 us
  transfers between devices with their start and end apart: 19, of which 19 were waited for; matrix products, arithmetic and copies ran while one was open for 5% of the time, Pallas kernels for 0%

profile of v1, /device:TPU:0, one launch (start us, length us, event | category | flops | bytes accessed | tf_op | source)
XLA Modules:
  0.0 1422.9 jit_solution(14408166346601009069)
XLA Ops:
  10.8 1174.8 %while.6 = (s32[]{:T(128)}, f32[3,1024,256]{1,2,0:T(8,128)}, f32[3,256]{1,0:T(4,128)}, f32[256,1024]{1,0:T(8,128)}, f32[1024,1024]{1,0:T(8,128)}, /*index=5*/f32...) while((s32[]{:T(128)}, f32[3,1024,256]{1,2,0:T(8,128)}, ...), condition=%wide.region_26.27_spmd.clone, body=%wide.region_0.26_spmd.clone.sunk | while | flops 23216961536 | bytes 635246848 | solution.py:351
  17.6 44.3 %all-gather.5.cloned.1.call-done = bf16[1,1024,1024]{2,1,0:T(8,128)(2,1)} async-done(((bf16[1,256,1024]{2,1,0:T(8,128)(2,1)}), bf16[1,1024,1024]{2,1,0:T(8,128)(2,1)}) %all-gather.5.cloned.1.call-update) | async-done | bytes 2097168 | tf_op jit(solution)/shard_map/while/body/eval_jaxpr/all_gather | solution.py:148
  74.1 8.8 fusion.227
  95.0 75.3 %reduce-scatter.5.cloned.1.call-done = f32[256,1024]{1,0:T(8,128)} async-done(((f32[1024,1024]{1,0:T(8,128)}), f32[256,1024]{1,0:T(8,128)}) %reduce-scatter.5.cloned.1.call-update) | async-done | bytes 1048592 | tf_op jit(solution)/shard_map/while/body/eval_jaxpr/reduce_scatter | solution.py:158
  173.1 46.6 %all-gather.7.cloned.1.call-done = bf16[1,1024,1024]{2,1,0:T(8,128)(2,1)} async-done(((bf16[1,256,1024]{2,1,0:T(8,128)(2,1)}), bf16[1,1024,1024]{2,1,0:T(8,128)(2,1)}) %all-gather.7.cloned.1.call-update) | async-done | bytes 2097168 | tf_op jit(solution)/shard_map/while/body/eval_jaxpr/all_gather | solution.py:171
  219.7 14.8 %multiply_convert_fusion.4 = (bf16[1024,1024]{1,0:T(8,128)(2,1)S(1)}, f32[1024,1024]{1,0:T(8,128)}, f32[1024,1024]{1,0:T(8,128)}) fusion(f32[1024]{0:T(1024)S(1)} %copy-done.58, bf16[1024,1024]{1,0:T(8,128)(2,1)} %get-tuple-element.1005, bf16[1,1024,1024]{2,1,0:T(8,128)(2,1)} %all-gather.7.cloned.1.call-done), kind=kOutput, calls=%fused_computation.17.clone.1 | convolution fusion | flops 2216689664 | bytes 14684160 | tf_op jit(solution)/shard_map/while/body/eval_jaxpr/gld,df->glf/dot_general | solution.py:173
  240.3 75.6 %reduce-scatter.7.cloned.1.call-done = f32[256,1024]{1,0:T(8,128)} async-done(((f32[1024,1024]{1,0:T(8,128)}), f32[256,1024]{1,0:T(8,128)}) %reduce-scatter.7.cloned.1.call-update) | async-done | bytes 1048592 | tf_op jit(solution)/shard_map/while/body/eval_jaxpr/reduce_scatter | solution.py:177
  322.0 46.0 %all-gather.9.cloned.1.call-done = bf16[1,1024,1024]{2,1,0:T(8,128)(2,1)} async-done(((bf16[1,256,1024]{2,1,0:T(8,128)(2,1)}), bf16[1,1024,1024]{2,1,0:T(8,128)(2,1)}) %all-gather.9.cloned.1.call-update) | async-done | bytes 2097168 | tf_op jit(solution)/shard_map/while/body/eval_jaxpr/all_gather | solution.py:204
  382.2 75.6 %reduce-scatter.9.cloned.1.call-done = f32[256,1024]{1,0:T(8,128)} async-done(((f32[1024,1024]{1,0:T(8,128)}), f32[256,1024]{1,0:T(8,128)}) %reduce-scatter.9.cloned.1.call-update) | async-done | bytes 1048592 | tf_op jit(solution)/shard_map/while/body/eval_jaxpr/reduce_scatter | solution.py:217
  461.6 46.5 %all-gather.11.cloned.1.call-done = bf16[1,1024,1024]{2,1,0:T(8,128)(2,1)} async-done(((bf16[1,256,1024]{2,1,0:T(8,128)(2,1)}), bf16[1,1024,1024]{2,1,0:T(8,128)(2,1)}) %all-gather.11.cloned.1.call-update) | async-done | bytes 2097168 | tf_op jit(solution)/shard_map/while/body/eval_jaxpr/all_gather | solution.py:234
  510.5 8.7 fusion.236
  519.3 11.8 multiply_reduce_fusion.18
  531.1 12.2 multiply_convert_fusion.5
  576.3 19.7 %reduce-scatter.11.cloned.1.call-done = bf16[256,1024]{1,0:T(8,128)(2,1)} async-done(((bf16[1024,1024]{1,0:T(8,128)(2,1)}), bf16[256,1024]{1,0:T(8,128)(2,1)}) %reduce-scatter.11.cloned.1.call-update) | async-done | bytes 524304 | tf_op jit(solution)/shard_map/while/body/eval_jaxpr/reduce_scatter | solution.py:256
  605.3 40.9 %all-gather.5.cloned.1.call-done = bf16[1,1024,1024]{2,1,0:T(8,128)(2,1)} async-done(((bf16[1,256,1024]{2,1,0:T(8,128)(2,1)}), bf16[1,1024,1024]{2,1,0:T(8,128)(2,1)}) %all-gather.5.cloned.1.call-update) | async-done | bytes 2097168 | tf_op jit(solution)/shard_map/while/body/eval_jaxpr/all_gather | solution.py:148
  658.4 8.8 fusion.227
  679.4 75.1 %reduce-scatter.5.cloned.1.call-done = f32[256,1024]{1,0:T(8,128)} async-done(((f32[1024,1024]{1,0:T(8,128)}), f32[256,1024]{1,0:T(8,128)}) %reduce-scatter.5.cloned.1.call-update) | async-done | bytes 1048592 | tf_op jit(solution)/shard_map/while/body/eval_jaxpr/reduce_scatter | solution.py:158
  757.4 46.5 %all-gather.7.cloned.1.call-done = bf16[1,1024,1024]{2,1,0:T(8,128)(2,1)} async-done(((bf16[1,256,1024]{2,1,0:T(8,128)(2,1)}), bf16[1,1024,1024]{2,1,0:T(8,128)(2,1)}) %all-gather.7.cloned.1.call-update) | async-done | bytes 2097168 | tf_op jit(solution)/shard_map/while/body/eval_jaxpr/all_gather | solution.py:171
  804.0 14.8 %multiply_convert_fusion.4 = (bf16[1024,1024]{1,0:T(8,128)(2,1)S(1)}, f32[1024,1024]{1,0:T(8,128)}, f32[1024,1024]{1,0:T(8,128)}) fusion(f32[1024]{0:T(1024)S(1)} %copy-done.58, bf16[1024,1024]{1,0:T(8,128)(2,1)} %get-tuple-element.1005, bf16[1,1024,1024]{2,1,0:T(8,128)(2,1)} %all-gather.7.cloned.1.call-done), kind=kOutput, calls=%fused_computation.17.clone.1 | convolution fusion | flops 2216689664 | bytes 14684160 | tf_op jit(solution)/shard_map/while/body/eval_jaxpr/gld,df->glf/dot_general | solution.py:173
  824.5 75.6 %reduce-scatter.7.cloned.1.call-done = f32[256,1024]{1,0:T(8,128)} async-done(((f32[1024,1024]{1,0:T(8,128)}), f32[256,1024]{1,0:T(8,128)}) %reduce-scatter.7.cloned.1.call-update) | async-done | bytes 1048592 | tf_op jit(solution)/shard_map/while/body/eval_jaxpr/reduce_scatter | solution.py:177
  905.9 46.4 %all-gather.9.cloned.1.call-done = bf16[1,1024,1024]{2,1,0:T(8,128)(2,1)} async-done(((bf16[1,256,1024]{2,1,0:T(8,128)(2,1)}), bf16[1,1024,1024]{2,1,0:T(8,128)(2,1)}) %all-gather.9.cloned.1.call-update) | async-done | bytes 2097168 | tf_op jit(solution)/shard_map/while/body/eval_jaxpr/all_gather | solution.py:204
  966.5 75.6 %reduce-scatter.9.cloned.1.call-done = f32[256,1024]{1,0:T(8,128)} async-done(((f32[1024,1024]{1,0:T(8,128)}), f32[256,1024]{1,0:T(8,128)}) %reduce-scatter.9.cloned.1.call-update) | async-done | bytes 1048592 | tf_op jit(solution)/shard_map/while/body/eval_jaxpr/reduce_scatter | solution.py:217
  1045.9 46.5 %all-gather.11.cloned.1.call-done = bf16[1,1024,1024]{2,1,0:T(8,128)(2,1)} async-done(((bf16[1,256,1024]{2,1,0:T(8,128)(2,1)}), bf16[1,1024,1024]{2,1,0:T(8,128)(2,1)}) %all-gather.11.cloned.1.call-update) | async-done | bytes 2097168 | tf_op jit(solution)/shard_map/while/body/eval_jaxpr/all_gather | solution.py:234
  1103.5 11.8 multiply_reduce_fusion.18
  1115.4 12.3 multiply_convert_fusion.5
  1162.8 17.5 %reduce-scatter.11.cloned.1.call-done = bf16[256,1024]{1,0:T(8,128)(2,1)} async-done(((bf16[1024,1024]{1,0:T(8,128)(2,1)}), bf16[256,1024]{1,0:T(8,128)(2,1)}) %reduce-scatter.11.cloned.1.call-update) | async-done | bytes 524304 | tf_op jit(solution)/shard_map/while/body/eval_jaxpr/reduce_scatter | solution.py:256
  1197.2 47.1 %all-reduce.8.cloned.1.call-done = f32[1024,288]{0,1:T(8,128)} async-done(((f32[1024,288]{0,1:T(8,128)}), f32[1024,288]{0,1:T(8,128)}) %all-reduce.8.cloned.1.call-update) | async-done | bytes 1179664 | tf_op jit(solution)/shard_map/psum | solution.py:357
  1244.4 13.2 all-reduce.2
  1258.8 17.9 %all-reduce.1 = (f32[1024]{0:T(1024)S(1)}, f32[1024]{0:T(1024)S(1)}, f32[1024]{0:T(1024)S(1)}, f32[1024]{0:T(1024)S(1)}, f32[1024]{0:T(1024)S(1)}, /*index=5*/f32[1024]{0:T(1024)S(1)}) all-reduce(f32[1024]{0:T(1024)S(1)} %copy-done.49, f32[1024]{0:T(1024)S(1)} %copy-done.46, ...), channel_id=1, replica_groups=mesh['dp'=8,'tensor'=4] {'tensor'}, use_global_device_ids=true, to_apply=%region_30.31 | all-reduce | flops 6144 | bytes 49152 | tf_op jit(solution)/shard_map/psum | solution.py:357
  1276.7 23.3 %all-reduce = (f32[1024]{0:T(1024)}, f32[1024]{0:T(1024)}, f32[1024]{0:T(1024)}, f32[1024]{0:T(1024)}, f32[1024]{0:T(1024)}, /*index=5*/f32[1024]{0:T(1024)}) all-reduce(f32[1024]{0:T(1024)S(1)} %get-tuple-element.525, f32[1024]{0:T(1024)S(1)} %get-tuple-element.526, ...), channel_id=1, replica_groups=mesh['dp'=8,'tensor'=4] {'dp'}, use_global_device_ids=true, to_apply=%region_31.32 | all-reduce | flops 6144 | bytes 49152 | tf_op jit(solution)/shard_map/psum | solution.py:357
  1300.1 52.7 %all-reduce.12.cloned.1.call-done = (bf16[3,1024,256]{2,1,0:T(8,128)(2,1)}, bf16[256,1024]{1,0:T(8,128)(2,1)}, bf16[1024,1024]{1,0:T(8,128)(2,1)}, bf16[1024,1024]{1,0:T(8,128)(2,1)}) async-done(((bf16[3,1024,256]{2,1,0:T(8,128)(2,1)}, bf16[256,1024]{1,0:T(8,128)(2,1)}, bf16[1024,1024]{1,0:T(8,128)(2,1)}, bf16[1024,1024]{1,0:T(8,128)(2,1)}), (bf16[3,1024,256]{2,1,0:T(8,128)(2,1)}, ...) | async-done | bytes 6291472 | tf_op jit(solution)/shard_map/psum | solution.py:355
  1363.3 49.5 %all-reduce.10.cloned.1.call-done = f32[1024,288]{0,1:T(8,128)} async-done(((f32[1024,288]{0,1:T(8,128)}), f32[1024,288]{0,1:T(8,128)}) %all-reduce.10.cloned.1.call-update) | async-done | bytes 1179664 | tf_op jit(solution)/shard_map/psum | solution.py:357
  (433 shorter events, 240.3 us)
Async XLA Ops:
  10.8 51.1 %all-gather.5.cloned.1.call-start = ((), (), s32[]{:S(2)}) async-start(), calls=%async_computation.7 | async-start | bytes 2621440 | tf_op jit(solution)/shard_map/while/body/eval_jaxpr/all_gather | solution.py:148
  12.7 157.6 %reduce-scatter.5.cloned.1.call-start = ((), (), s32[]{:S(2)}) async-start(), calls=%async_computation.8 | async-start | bytes 5242880 | tf_op jit(solution)/shard_map/while/body/eval_jaxpr/reduce_scatter | solution.py:158
  94.6 75.7 %copy-start.17 = (bf16[2,256,1024]{2,1,0:T(8,128)(2,1)S(1)}, bf16[2,256,1024]{2,1,0:T(8,128)(2,1)}, u32[]{:S(2)}) copy-start(bf16[2,256,1024]{2,1,0:T(8,128)(2,1)} %get-tuple-element.998) | copy-start | bytes 3145732 | tf_op jit(solution)/shard_map/while
  94.6 75.7 %copy-start.50 = (f32[1024]{0:T(1024)S(1)}, f32[1024]{0:T(1024)}, u32[]{:S(2)}) copy-start(f32[1024]{0:T(1024)} %get-tuple-element.1002) | copy-start | bytes 12292 | tf_op jit(solution)/shard_map/while
  94.6 77.4 %copy-start.28 = (f32[1024]{0:T(1024)S(1)}, f32[1024]{0:T(1024)}, u32[]{:S(2)}) copy-start(f32[1024]{0:T(1024)} %get-tuple-element.1003) | copy-start | bytes 12292 | tf_op jit(solution)/shard_map/while
  94.6 77.4 %copy-start.30 = (f32[1024]{0:T(1024)S(1)}, f32[1024]{0:T(1024)}, u32[]{:S(2)}) copy-start(f32[1024]{0:T(1024)} %get-tuple-element.1004) | copy-start | bytes 12292 | tf_op jit(solution)/shard_map/while
  94.6 125.1 %copy-start.58 = (f32[1024]{0:T(1024)S(1)}, f32[1024]{0:T(1024)}, u32[]{:S(2)}) copy-start(f32[1024]{0:T(1024)} %get-tuple-element.1006) | copy-start | bytes 12292 | tf_op jit(solution)/shard_map/while
  94.6 125.1 %all-gather.7.cloned.1.call-start = ((), (), s32[]{:S(2)}) async-start(), calls=%async_computation.9 | async-start | bytes 2621440 | tf_op jit(solution)/shard_map/while/body/eval_jaxpr/all_gather | solution.py:171
  173.1 142.7 %reduce-scatter.7.cloned.1.call-start = ((), (), s32[]{:S(2)}) async-start(), calls=%async_computation.10 | async-start | bytes 5242880 | tf_op jit(solution)/shard_map/while/body/eval_jaxpr/reduce_scatter | solution.py:177
  240.2 75.7 %copy-start.51 = (f32[1024]{0:T(1024)S(1)}, f32[1024]{0:T(1024)}, u32[]{:S(2)}) copy-start(f32[1024]{0:T(1024)} %get-tuple-element.1008) | copy-start | bytes 12292 | tf_op jit(solution)/shard_map/while
  240.2 77.6 %copy-start.31 = (f32[1024]{0:T(1024)S(1)}, f32[1024]{0:T(1024)}, u32[]{:S(2)}) copy-start(f32[1024]{0:T(1024)} %get-tuple-element.1012) | copy-start | bytes 12292 | tf_op jit(solution)/shard_map/while
  240.2 127.8 %all-gather.9.cloned.1.call-start = ((), (), s32[]{:S(2)}) async-start(), calls=%async_computation.11 | async-start | bytes 2621440 | tf_op jit(solution)/shard_map/while/body/eval_jaxpr/all_gather | solution.py:204
  321.4 136.4 %reduce-scatter.9.cloned.1.call-start = ((), (), s32[]{:S(2)}) async-start(), calls=%async_computation.12 | async-start | bytes 5242880 | tf_op jit(solution)/shard_map/while/body/eval_jaxpr/reduce_scatter | solution.py:217
  382.2 125.9 %all-gather.11.cloned.1.call-start = ((), (), s32[]{:S(2)}) async-start(), calls=%async_computation.13 | async-start | bytes 2621440 | tf_op jit(solution)/shard_map/while/body/eval_jaxpr/all_gather | solution.py:234
  461.5 134.5 %reduce-scatter.11.cloned.1.call-start = ((), (), s32[]{:S(2)}) async-start(), calls=%async_computation.14 | async-start | bytes 2621440 | tf_op jit(solution)/shard_map/while/body/eval_jaxpr/reduce_scatter | solution.py:256
  598.4 47.7 %all-gather.5.cloned.1.call-start = ((), (), s32[]{:S(2)}) async-start(), calls=%async_computation.7 | async-start | bytes 2621440 | tf_op jit(solution)/shard_map/while/body/eval_jaxpr/all_gather | solution.py:148
  600.4 154.1 %reduce-scatter.5.cloned.1.call-start = ((), (), s32[]{:S(2)}) async-start(), calls=%async_computation.8 | async-start | bytes 5242880 | tf_op jit(solution)/shard_map/while/body/eval_jaxpr/reduce_scatter | solution.py:158
  678.8 75.7 %copy-start.17 = (bf16[2,256,1024]{2,1,0:T(8,128)(2,1)S(1)}, bf16[2,256,1024]{2,1,0:T(8,128)(2,1)}, u32[]{:S(2)}) copy-start(bf16[2,256,1024]{2,1,0:T(8,128)(2,1)} %get-tuple-element.998) | copy-start | bytes 3145732 | tf_op jit(solution)/shard_map/while
  678.9 75.7 %copy-start.50 = (f32[1024]{0:T(1024)S(1)}, f32[1024]{0:T(1024)}, u32[]{:S(2)}) copy-start(f32[1024]{0:T(1024)} %get-tuple-element.1002) | copy-start | bytes 12292 | tf_op jit(solution)/shard_map/while
  678.9 77.4 %copy-start.28 = (f32[1024]{0:T(1024)S(1)}, f32[1024]{0:T(1024)}, u32[]{:S(2)}) copy-start(f32[1024]{0:T(1024)} %get-tuple-element.1003) | copy-start | bytes 12292 | tf_op jit(solution)/shard_map/while
  678.9 77.4 %copy-start.30 = (f32[1024]{0:T(1024)S(1)}, f32[1024]{0:T(1024)}, u32[]{:S(2)}) copy-start(f32[1024]{0:T(1024)} %get-tuple-element.1004) | copy-start | bytes 12292 | tf_op jit(solution)/shard_map/while
  678.9 125.1 %copy-start.58 = (f32[1024]{0:T(1024)S(1)}, f32[1024]{0:T(1024)}, u32[]{:S(2)}) copy-start(f32[1024]{0:T(1024)} %get-tuple-element.1006) | copy-start | bytes 12292 | tf_op jit(solution)/shard_map/while
  678.9 125.1 %all-gather.7.cloned.1.call-start = ((), (), s32[]{:S(2)}) async-start(), calls=%async_computation.9 | async-start | bytes 2621440 | tf_op jit(solution)/shard_map/while/body/eval_jaxpr/all_gather | solution.py:171
  757.4 142.7 %reduce-scatter.7.cloned.1.call-start = ((), (), s32[]{:S(2)}) async-start(), calls=%async_computation.10 | async-start | bytes 5242880 | tf_op jit(solution)/shard_map/while/body/eval_jaxpr/reduce_scatter | solution.py:177
  824.4 77.6 %copy-start.31 = (f32[1024]{0:T(1024)S(1)}, f32[1024]{0:T(1024)}, u32[]{:S(2)}) copy-start(f32[1024]{0:T(1024)} %get-tuple-element.1012) | copy-start | bytes 12292 | tf_op jit(solution)/shard_map/while
  824.5 127.8 %all-gather.9.cloned.1.call-start = ((), (), s32[]{:S(2)}) async-start(), calls=%async_computation.11 | async-start | bytes 2621440 | tf_op jit(solution)/shard_map/while/body/eval_jaxpr/all_gather | solution.py:204
  905.6 136.4 %reduce-scatter.9.cloned.1.call-start = ((), (), s32[]{:S(2)}) async-start(), calls=%async_computation.12 | async-start | bytes 5242880 | tf_op jit(solution)/shard_map/while/body/eval_jaxpr/reduce_scatter | solution.py:217
  966.4 125.9 %all-gather.11.cloned.1.call-start = ((), (), s32[]{:S(2)}) async-start(), calls=%async_computation.13 | async-start | bytes 2621440 | tf_op jit(solution)/shard_map/while/body/eval_jaxpr/all_gather | solution.py:234
  1045.8 134.6 %reduce-scatter.11.cloned.1.call-start = ((), (), s32[]{:S(2)}) async-start(), calls=%async_computation.14 | async-start | bytes 2621440 | tf_op jit(solution)/shard_map/while/body/eval_jaxpr/reduce_scatter | solution.py:256
  1185.6 58.7 %all-reduce.8.cloned.1.call-start = ((), (), s32[]{:S(2)}) async-start(), calls=%async_computation.4 | async-start | bytes 2359296 | tf_op jit(solution)/shard_map/psum | solution.py:357
  1186.2 166.6 %all-reduce.12.cloned.1.call-start = ((), (), s32[]{:S(2)}) async-start(), calls=%async_computation.6 | async-start | bytes 12582912 | tf_op jit(solution)/shard_map/psum | solution.py:355
  1197.1 215.7 %all-reduce.10.cloned.1.call-start = ((), (), s32[]{:S(2)}) async-start(), calls=%async_computation.5 | async-start | bytes 2359296 | tf_op jit(solution)/shard_map/psum | solution.py:357
  (102 other events, 1052.8 us)
Sparse Core Ops, SparseCore 0:
  13.2 48.6 all-gather.4
  94.7 75.4 reduce-scatter.4
  173.2 46.4 all-gather.6
  240.3 75.4 reduce-scatter.6
  321.5 46.4 all-gather.8
  382.3 75.4 reduce-scatter.8
  461.6 46.4 all-gather.10
  553.4 42.5 reduce-scatter.10
  600.8 45.2 all-gather.4
  679.0 75.4 reduce-scatter.4
  757.5 46.4 all-gather.6
  824.6 75.4 reduce-scatter.6
  905.8 46.4 all-gather.8
  966.5 75.4 reduce-scatter.8
  1045.9 46.4 all-gather.10
  1137.7 42.5 reduce-scatter.10
Sparse Core Ops, SparseCore 1:
  1189.0 55.2 all-reduce.7
  1249.0 103.7 all-reduce.11
  1356.1 56.7 all-reduce.9
